TPU v7x, 32 devices: a whole 2x2x4 slice. The times are simulated.
32 devices in a mesh: seq: 8 (over z, core), fsdp: 4 (over y, x).
Axes of the slice: x: 2, y: 2, z: 4, core: 2. Of those that a mesh axis runs over, the one named last changes fastest.
Arguments:
- signal: bfloat16 [4, 8192, 1024], P('fsdp', 'seq'), may hold values from -6 to 6
- cotangent: bfloat16 [4, 8192, 1024], P('fsdp', 'seq'), may hold values from -6 to 6
- w_in: bfloat16 [1024, 1024], P('fsdp'), may hold values from -0.1875 to 0.1875
- w_conv: bfloat16 [2, 1024, 128], P(None, 'seq'), may hold values from -0.5 to 0.5
- w_out: bfloat16 [1024, 1024], P('fsdp'), may hold values from -0.1875 to 0.1875
- dilation: int32 [16], P('seq'), may hold values from 512 to 4095
- lengths: int32 [4], P('fsdp'), may hold values from 2048 to 8192, as said below
Outputs:
- grad_signal: bfloat16 [4, 8192, 1024], P('fsdp', 'seq')
- grad_in: float32 [1024, 1024], P('fsdp')
- grad_out: float32 [1024, 1024], P('fsdp')
- grad_conv: float32 [2, 1024, 128], P(None, 'seq')
Inputs may be any that keep to these rules, and one draw needn't show every extreme that they name: `lengths`: some record in every draw holds all 8192 samples.
All inputs are finite; a program needn't handle non-finite values.
Results may differ from a plain program's by a relative error of at most 0.0068.
Values may be sent and summed in bfloat16 or wider, within the bound.
No kernel may reach another device: no remote copies, remote signals or barrier semaphores. Data moves between devices by JAX's collectives and lax.ppermute only.
A program may use at most 128 MiB of HBM per device.

v0:
```python
import math
import jax
import jax.numpy as jnp
from jax import lax
from jax.sharding import PartitionSpec as P


def delayed(series, amount):
    padded = jnp.concatenate([jnp.zeros_like(series), series], axis=0)
    return lax.dynamic_slice_in_dim(padded, series.shape[0] - amount, series.shape[0], 0)


def advanced(series, amount):
    padded = jnp.concatenate([series, jnp.zeros_like(series)], axis=0)
    return lax.dynamic_slice_in_dim(padded, amount, series.shape[0], 0)


def group_pass(projected, grad_gated, kernel, amount, live_mask):
    group_width = kernel.shape[0] // 2
    stacked = jnp.concatenate([projected, delayed(projected, amount)], axis=1)
    pre_acts = jnp.dot(stacked, kernel, preferred_element_type=jnp.float32)
    tanh_act = jnp.tanh(pre_acts[:, :group_width])
    sig_act = jax.nn.sigmoid(pre_acts[:, group_width:])
    masked = live_mask[:, None]
    gated_out = (tanh_act * sig_act * masked).astype(jnp.bfloat16)
    grad_masked = grad_gated.astype(jnp.float32) * masked
    grad_filter = grad_masked * sig_act * (1.0 - tanh_act * tanh_act)
    grad_gate = grad_masked * tanh_act * sig_act * (1.0 - sig_act)
    grad_acts = jnp.concatenate([grad_filter, grad_gate], axis=1).astype(jnp.bfloat16)
    grad_kernel = jnp.dot(stacked.T, grad_acts, preferred_element_type=jnp.float32)
    paired = jnp.concatenate([grad_acts, advanced(grad_acts, amount)], axis=1)
    back_kernel = jnp.concatenate([kernel[:group_width].T, kernel[group_width:].T], axis=0)
    grad_mixed = jnp.dot(paired, back_kernel, preferred_element_type=jnp.float32).astype(
        jnp.bfloat16
    )
    return (gated_out, grad_mixed, grad_kernel)


def column_order(series, fsdp_size, seq_size):
    samples, channels = series.shape
    quarter = channels // (fsdp_size * seq_size)
    return (
        series.reshape(samples, fsdp_size, seq_size, quarter)
        .transpose(0, 2, 1, 3)
        .reshape(samples, channels)
    )


def outer_terms(left_side, right_side):
    return lax.dot_general(
        left_side, right_side, (((0,), (0,)), ((), ())), preferred_element_type=jnp.float32
    )


def local(signal, cotangent, w_in, w_conv, w_out, dilation, lengths):
    record = signal[0]
    upstream = cotangent[0]
    samples, channels = record.shape
    seq_size = lax.axis_size("seq")
    fsdp_size = lax.axis_size("fsdp")
    full_len = samples * seq_size
    local_groups = dilation.shape[0]
    local_chans = w_conv.shape[1]
    group_width = local_chans // local_groups
    factor = 1.0 / math.sqrt(full_len * fsdp_size)
    projected = jnp.dot(
        record, lax.all_gather(w_in, "fsdp", axis=0, tiled=True), preferred_element_type=jnp.float32
    ).astype(jnp.bfloat16)
    grad_gated = lax.dot_general(
        upstream,
        lax.all_gather(w_out, "fsdp", axis=0, tiled=True),
        (((1,), (1,)), ((), ())),
        preferred_element_type=jnp.float32,
    ).astype(jnp.bfloat16)
    proj_groups, grad_groups = (
        lax.all_to_all(projected, "seq", split_axis=1, concat_axis=0, tiled=True),
        lax.all_to_all(grad_gated, "seq", split_axis=1, concat_axis=0, tiled=True),
    )
    live_mask = (jnp.arange(full_len, dtype=jnp.int32) < lengths[0]).astype(jnp.float32)
    gated_parts = []
    mixed_parts = []
    tap_zero = []
    tap_one = []
    for group_index in range(local_groups):
        low_chan = group_index * group_width
        kernel = jnp.concatenate(
            [
                w_conv[0, low_chan : low_chan + group_width],
                w_conv[1, low_chan : low_chan + group_width],
            ],
            axis=0,
        )
        gated_out, grad_mixed, grad_kernel = group_pass(
            proj_groups[:, low_chan : low_chan + group_width],
            grad_groups[:, low_chan : low_chan + group_width],
            kernel,
            dilation[group_index],
            live_mask,
        )
        gated_parts.append(gated_out)
        mixed_parts.append(grad_mixed)
        tap_zero.append(grad_kernel[:group_width])
        tap_one.append(grad_kernel[group_width:])
    gated_groups = jnp.concatenate(gated_parts, axis=1)
    mixed_groups = jnp.concatenate(mixed_parts, axis=1)
    conv_local = jnp.stack(
        [jnp.concatenate(tap_zero, axis=0), jnp.concatenate(tap_one, axis=0)], axis=0
    )
    conv_total = lax.psum(conv_local, "fsdp")
    gated_time, mixed_time = (
        lax.all_to_all(gated_groups, "seq", split_axis=0, concat_axis=1, tiled=True),
        lax.all_to_all(mixed_groups, "seq", split_axis=0, concat_axis=1, tiled=True),
    )
    mixed_back = lax.dot_general(
        mixed_time,
        lax.all_gather(w_in, "fsdp", axis=0, tiled=True),
        (((1,), (1,)), ((), ())),
        preferred_element_type=jnp.float32,
    )
    grad_signal = (upstream.astype(jnp.float32) + mixed_back).astype(jnp.bfloat16)[None]
    gated_order = column_order(gated_time, fsdp_size, seq_size)
    record_order = column_order(record, fsdp_size, seq_size)
    part_out = lax.psum_scatter(
        outer_terms(gated_order, upstream), ("seq", "fsdp"), scatter_dimension=0, tiled=True
    )
    part_in = lax.psum_scatter(
        outer_terms(record_order, mixed_time), ("seq", "fsdp"), scatter_dimension=0, tiled=True
    )
    grad_in, grad_out = (
        lax.all_gather(part_in, "seq", axis=0, tiled=True),
        lax.all_gather(part_out, "seq", axis=0, tiled=True),
    )
    return (grad_signal, grad_in * factor, grad_out * factor, conv_total * factor)


def solution(mesh):
    placed = (
        P("fsdp", "seq", None),
        P("fsdp", "seq", None),
        P("fsdp", None),
        P(None, "seq", None),
        P("fsdp", None),
        P("seq"),
        P("fsdp"),
    )
    return jax.shard_map(
        local,
        mesh=mesh,
        in_specs=placed,
        out_specs=(P("fsdp", "seq", None), P("fsdp", None), P("fsdp", None), P(None, "seq", None)),
        check_vma=False,
    )
```

profile of v0, /device:TPU:0, one launch (start us, length us, event | category | flops | bytes accessed | tf_op | source)
XLA Modules:
  0.0 627.7 jit_solution(6793822717476289242)
XLA Ops:
  8.6 39.1 %all-gather.7.cloned.1.call-done = bf16[1024,1024]{1,0:T(8,128)(2,1)} async-done(((bf16[256,1024]{1,0:T(8,128)(2,1)}), bf16[1024,1024]{1,0:T(8,128)(2,1)}) %all-gather.7.cloned.1.call-update) | async-done | bytes 2097168 | tf_op jit(solution)/shard_map/all_gather | solution.py:67
  47.8 4.6 fusion.26
  52.4 2.4 copy.26
  54.7 4.6 all-to-all-start.1
  59.3 25.5 %all-gather.5.cloned.1.call-done = bf16[1024,1024]{1,0:T(8,128)(2,1)} async-done(((bf16[256,1024]{1,0:T(8,128)(2,1)}), bf16[1024,1024]{1,0:T(8,128)(2,1)}) %all-gather.5.cloned.1.call-update) | async-done | bytes 2097168 | tf_op jit(solution)/shard_map/all_gather | solution.py:71
  84.8 6.0 fusion.23
  90.8 17.6 %all-to-all-done.1 = bf16[1024,8,128]{2,0,1:T(8,128)(2,1)S(1)} async-done(((bf16[1024,8,128]{2,0,1:T(8,128)(2,1)}), bf16[1024,8,128]{2,0,1:T(8,128)(2,1)S(1)}, u32[]{:S(2)}, u32[]{:S(2)}) %all-to-all-start.1) | async-done | bytes 2097184 | tf_op jit(solution)/shard_map/all_to_all | solution.py:76
  108.4 4.7 all-to-all-start
  116.7 2.7 fusion.52
  119.4 42.5 %all-to-all-done = bf16[1024,8,128]{0,2,1:T(8,128)(2,1)} async-done(((bf16[1024,8,128]{0,2,1:T(8,128)(2,1)}), bf16[1024,8,128]{0,2,1:T(8,128)(2,1)}, u32[]{:S(2)}, u32[]{:S(2)}) %all-to-all-start) | async-done | bytes 2097184 | tf_op jit(solution)/shard_map/all_to_all | solution.py:77
  164.8 8.6 %pad_dynamic-slice_fusion.1 = (bf16[8192,64]{1,0:T(8,128)(2,1)S(1)}, bf16[8192,64]{1,0:T(8,128)(2,1)S(1)}) fusion(s32[]{:T(128)S(6)} %select_n.14, bf16[8192,64]{1,0:T(8,128)(2,1)S(1)} %copy-done, s32[]{:T(128)S(6)} %select_n.12, bf16[8192,64]{1,0:T(8,128)(2,1)S(1)} %copy-done.1), kind=kLoop, calls=%fused_computation.14 | loop fusion | bytes 4194312 | tf_op jit(solution)/shard_map/dynamic_slice | solution.py:10
  176.9 3.7 multiply_convert_fusion.3
  182.3 4.3 all-to-all-start.3
  190.3 3.1 pad_maximum_fusion.1
  193.4 42.3 %all-to-all-done.3 = bf16[8,1024,128]{1,2,0:T(8,128)(2,1)} async-done(((bf16[8,1024,128]{1,2,0:T(8,128)(2,1)}), bf16[8,1024,128]{1,2,0:T(8,128)(2,1)}, u32[]{:S(2)}, u32[]{:S(2)}) %all-to-all-start.3) | async-done | bytes 2097184 | tf_op jit(solution)/shard_map/all_to_all | solution.py:111
  237.9 4.3 fusion.19
  242.3 2.4 pad_dynamic-slice_fusion.2
  249.8 4.4 all-to-all-start.2
  254.2 4.0 copy.28
  258.2 3.3 copy.29
  261.4 49.1 %all-to-all-done.2 = bf16[8,1024,128]{1,2,0:T(8,128)(2,1)} async-done(((bf16[8,1024,128]{1,2,0:T(8,128)(2,1)}), bf16[8,1024,128]{1,2,0:T(8,128)(2,1)}, u32[]{:S(2)}, u32[]{:S(2)}) %all-to-all-start.2) | async-done | bytes 2097184 | tf_op jit(solution)/shard_map/all_to_all | solution.py:112
  310.5 6.6 %convolution_bitcast_fusion = f32[1024,1024]{0,1:T(8,128)} fusion(bf16[1024,1024]{0,1:T(8,128)(2,1)} %bitcast.20, bf16[1024,1024]{0,1:T(8,128)(2,1)} %bitcast.91), kind=kOutput, calls=%fused_computation.17 | convolution fusion | flops 2147483648 | bytes 8388608 | tf_op jit(solution)/shard_map/dot_general | solution.py:50
  317.1 5.5 copy.36
  323.0 4.5 fusion.31
  329.9 56.5 %reduce-scatter.9.cloned.1.call-done = f32[32,1024]{1,0:T(8,128)} async-done(((f32[1024,1024]{1,0:T(8,128)}), f32[32,1024]{1,0:T(8,128)}) %reduce-scatter.9.cloned.1.call-update) | async-done | bytes 131088 | tf_op jit(solution)/shard_map/reduce_scatter | solution.py:123
  386.5 142.3 %reduce-scatter.7.cloned.1.call-done = f32[32,1024]{1,0:T(8,128)} async-done(((f32[1024,1024]{1,0:T(8,128)}), f32[32,1024]{1,0:T(8,128)}) %reduce-scatter.7.cloned.1.call-update) | async-done | bytes 131088 | tf_op jit(solution)/shard_map/reduce_scatter | solution.py:126
  528.8 42.5 %all-reduce.6.cloned.1.call-done = f32[2,128,128]{2,1,0:T(8,128)} async-done(((f32[2,128,128]{2,1,0:T(8,128)}), f32[2,128,128]{2,1,0:T(8,128)}) %all-reduce.6.cloned.1.call-update) | async-done | bytes 131088 | tf_op jit(solution)/shard_map/psum | solution.py:109
  572.9 6.6 %fusion.10 = bf16[1,1024,1024]{2,1,0:T(8,128)(2,1)} fusion(bf16[1,1024,1024]{2,1,0:T(8,128)(2,1)} %param.8, bf16[1024,1024]{0,1:T(8,128)(2,1)} %bitcast.20, bf16[1024,1024]{1,0:T(8,128)(2,1)} %all-gather.7.cloned.1.call-done), kind=kOutput, calls=%fused_computation.18 | convolution fusion | flops 2150629376 | bytes 8388608 | tf_op jit(solution)/shard_map/dot_general | solution.py:114
  579.5 15.6 %all-gather.11.cloned.1.call-done = f32[256,1024]{1,0:T(8,128)} async-done(((f32[32,1024]{1,0:T(8,128)}), f32[256,1024]{1,0:T(8,128)}) %all-gather.11.cloned.1.call-update) | async-done | bytes 1048592 | tf_op jit(solution)/shard_map/all_gather | solution.py:131
  595.1 2.3 broadcast_multiply_fusion
  597.4 21.1 %all-gather.9.cloned.1.call-done = f32[256,1024]{1,0:T(8,128)} async-done(((f32[32,1024]{1,0:T(8,128)}), f32[256,1024]{1,0:T(8,128)}) %all-gather.9.cloned.1.call-update) | async-done | bytes 1048592 | tf_op jit(solution)/shard_map/all_gather | solution.py:130
  618.5 2.3 broadcast_multiply_fusion.1
  (60 shorter events, 21.7 us)
Async XLA Ops:
  7.2 40.6 %all-gather.7.cloned.1.call-start = ((), (), s32[]{:S(2)}) async-start(), calls=%async_computation.7 | async-start | bytes 2621440 | tf_op jit(solution)/shard_map/all_gather | solution.py:67
  7.9 76.9 %all-gather.5.cloned.1.call-start = ((), (), s32[]{:S(2)}) async-start(), calls=%async_computation.6 | async-start | bytes 2621440 | tf_op jit(solution)/shard_map/all_gather | solution.py:71
  54.7 53.6 %all-to-all-start.1 = ((bf16[1024,8,128]{2,0,1:T(8,128)(2,1)}), bf16[1024,8,128]{2,0,1:T(8,128)(2,1)S(1)}, u32[]{:S(2)}, u32[]{:S(2)}) async-start(bf16[1024,8,128]{2,0,1:T(8,128)(2,1)} %copy.26), calls=%async_computation.1 | async-start | bytes 4194304 | tf_op jit(solution)/shard_map/all_to_all | solution.py:76
  108.4 4.7 copy-start.10
  108.4 8.3 %copy-start.9 = (bf16[2,128,128]{2,1,0:T(8,128)(2,1)S(1)}, bf16[2,128,128]{2,1,0:T(8,128)(2,1)}, u32[]{:S(2)}) copy-start(bf16[2,128,128]{2,1,0:T(8,128)(2,1)} %param.10) | copy-start | bytes 196612
  108.4 53.5 %all-to-all-start = ((bf16[1024,8,128]{0,2,1:T(8,128)(2,1)}), bf16[1024,8,128]{0,2,1:T(8,128)(2,1)}, u32[]{:S(2)}, u32[]{:S(2)}) async-start(bf16[1024,8,128]{0,2,1:T(8,128)(2,1)} %bitcast.90), calls=%async_computation | async-start | bytes 4194304 | tf_op jit(solution)/shard_map/all_to_all | solution.py:77
  161.9 2.2 copy-start
  161.9 2.9 copy-start.1
  173.4 1.4 copy-start.4
  173.4 2.0 copy-start.2
  182.3 53.4 %all-to-all-start.3 = ((bf16[8,1024,128]{1,2,0:T(8,128)(2,1)}), bf16[8,1024,128]{1,2,0:T(8,128)(2,1)}, u32[]{:S(2)}, u32[]{:S(2)}) async-start(bf16[8,1024,128]{1,2,0:T(8,128)(2,1)} %bitcast.84), calls=%async_computation.3 | async-start | bytes 4194304 | tf_op jit(solution)/shard_map/all_to_all | solution.py:111
  186.7 199.8 %reduce-scatter.9.cloned.1.call-start = ((), (), s32[]{:S(2)}) async-start(), calls=%async_computation.12 | async-start | bytes 4325376 | tf_op jit(solution)/shard_map/reduce_scatter | solution.py:123
  235.7 2.2 copy-start.11
  242.3 2.5 copy-start.7
  242.3 2.5 copy-start.8
  244.7 1.2 copy-start.5
  249.8 60.8 %all-to-all-start.2 = ((bf16[8,1024,128]{1,2,0:T(8,128)(2,1)}), bf16[8,1024,128]{1,2,0:T(8,128)(2,1)}, u32[]{:S(2)}, u32[]{:S(2)}) async-start(bf16[8,1024,128]{1,2,0:T(8,128)(2,1)} %bitcast.85), calls=%async_computation.2 | async-start | bytes 4194304 | tf_op jit(solution)/shard_map/all_to_all | solution.py:112
  254.1 274.7 %reduce-scatter.7.cloned.1.call-start = ((), (), s32[]{:S(2)}) async-start(), calls=%async_computation.11 | async-start | bytes 4325376 | tf_op jit(solution)/shard_map/reduce_scatter | solution.py:126
  322.7 248.7 %all-reduce.6.cloned.1.call-start = ((), (), s32[]{:S(2)}) async-start(), calls=%async_computation.10 | async-start | bytes 262144 | tf_op jit(solution)/shard_map/psum | solution.py:109
  323.0 4.5 copy-start.3
  323.0 4.5 copy-start.6
  329.9 265.2 %all-gather.11.cloned.1.call-start = ((), (), s32[]{:S(2)}) async-start(), calls=%async_computation.9 | async-start | bytes 1179648 | tf_op jit(solution)/shard_map/all_gather | solution.py:131
  386.5 232.0 %all-gather.9.cloned.1.call-start = ((), (), s32[]{:S(2)}) async-start(), calls=%async_computation.8 | async-start | bytes 1179648 | tf_op jit(solution)/shard_map/all_gather | solution.py:130
Sparse Core Ops, SparseCore 0:
  9.8 37.8 all-gather.6
  49.6 35.1 all-gather.4
  242.4 144.0 reduce-scatter.8
  388.6 140.1 reduce-scatter.6
  532.1 39.1 all-reduce.5
  572.8 22.2 all-gather.10
  596.7 21.8 all-gather.8
where the time goes:
time: 629 us; the launch traced here: 628 us
  waiting for transfers between devices  496 us (79%)
  local copies, waits for them, and re-layouts  39.4 us (6%)
  matrix products  38.9 us (6%)
  between operations  21 us (3%)
  starting transfers between devices  18.5 us (3%)
  other arithmetic  14.3 us (2%)
    reduce_scatter x1, waiting for transfers between devices, local(): lax.psum_scatter(outer_terms(record_order, mixed_time), ('seq', 'fsdp'),...  142 us
    reduce_scatter x1, waiting for transfers between devices, local(): lax.psum_scatter(outer_terms(gated_order, upstream), ('seq', 'fsdp'), sca...  56.5 us
    all_to_all x1, waiting for transfers between devices, local(): lax.all_to_all(mixed_groups, 'seq', split_axis=0, concat_axis=1, tiled=True)  49.1 us
    psum x1, waiting for transfers between devices, local(): conv_total = lax.psum(conv_local, 'fsdp')  42.5 us
    all_to_all x1, waiting for transfers between devices, local(): lax.all_to_all(grad_gated, 'seq', split_axis=1, concat_axis=0, tiled=True)  42.5 us
    all_to_all x1, waiting for transfers between devices, local(): lax.all_to_all(gated_groups, 'seq', split_axis=0, concat_axis=1, tiled=True)  42.3 us
    all_gather x1, waiting for transfers between devices, local(): lax.all_gather(w_in, 'fsdp', axis=0, tiled=True)  39.1 us
    all_gather x1, waiting for transfers between devices, local(): lax.all_gather(w_out, 'fsdp', axis=0, tiled=True)  25.5 us
  transfers between devices with their start and end apart: 11, of which 11 were waited for; matrix products, arithmetic and copies ran while one was open for 10% of the time, Pallas kernels for 0%

commit v1 on v0

--- a/solution.py
+++ b/solution.py
@@ -1,8 +1,17 @@
+import functools
 import math
 import jax
 import jax.numpy as jnp
 from jax import lax
 from jax.sharding import PartitionSpec as P
+from jax.lax import all_gather
+
+
+def part_sums_all(field, along_axis):
+    return all_gather(field, axis_name=along_axis).sum(axis=0)
+
+
+heaps_plan = functools.partial(part_sums_all, along_axis="fsdp")
 
 
 def delayed(series, amount):
@@ -106,7 +115,7 @@
     conv_local = jnp.stack(
         [jnp.concatenate(tap_zero, axis=0), jnp.concatenate(tap_one, axis=0)], axis=0
     )
-    conv_total = lax.psum(conv_local, "fsdp")
+    conv_total = heaps_plan(conv_local)
     gated_time, mixed_time = (
         lax.all_to_all(gated_groups, "seq", split_axis=0, concat_axis=1, tiled=True),
         lax.all_to_all(mixed_groups, "seq", split_axis=0, concat_axis=1, tiled=True),

time: 629 us -> 582 us (0.925)
  waiting for transfers between devices: 496 us -> 441 us
  blocking collectives: 0 us -> 8.53 us
    psum x1 -> x0, waiting for transfers between devices: 42.5 us -> none  [local(): conv_total = lax.psum(conv_local, 'fsdp')]
    all_gather x1, waiting for transfers between devices: 15.6 us -> 4.05 us  [local(): lax.all_gather(part_out, 'seq', axis=0, tiled=True)]
    all_gather x0 -> x1, blocking collectives: none -> 8.53 us  [part_sums_all(): return all_gather(field, axis_name=along_axis).sum(axis=0)]
    reduce_scatter x1, waiting for transfers between devices: 56.5 us -> 63.7 us  [local(): lax.psum_scatter(outer_terms(gated_order, upstream), ('seq', 'fsdp'), sca...]
    reduce_scatter x1, waiting for transfers between devices: 142 us -> 136 us  [local(): lax.psum_scatter(outer_terms(record_order, mixed_time), ('seq', 'fsdp'),...]
  transfers between devices with their start and end apart: 11 -> 10, of which waited for: 11 -> 10; matrix products, arithmetic and copies ran while one was open for 10% -> 11% of each run, Pallas kernels for 0% -> 0%
where the time goes in v1:
time: 582 us; the launch traced here: 581 us
  waiting for transfers between devices  441 us (76%)
  local copies, waits for them, and re-layouts  39.5 us (7%)
  matrix products  38.9 us (7%)
  between operations  21.7 us (4%)
  starting transfers between devices  18.5 us (3%)
  other arithmetic  12.8 us (2%)
  blocking collectives  8.53 us (1%)
    reduce_scatter x1, waiting for transfers between devices, local(): lax.psum_scatter(outer_terms(record_order, mixed_time), ('seq', 'fsdp'),...  136 us
    reduce_scatter x1, waiting for transfers between devices, local(): lax.psum_scatter(outer_terms(gated_order, upstream), ('seq', 'fsdp'), sca...  63.7 us
    all_to_all x1, waiting for transfers between devices, local(): lax.all_to_all(mixed_groups, 'seq', split_axis=0, concat_axis=1, tiled=True)  49.1 us
    all_to_all x1, waiting for transfers between devices, local(): lax.all_to_all(grad_gated, 'seq', split_axis=1, concat_axis=0, tiled=True)  42.1 us
    all_to_all x1, waiting for transfers between devices, local(): lax.all_to_all(gated_groups, 'seq', split_axis=0, concat_axis=1, tiled=True)  41.9 us
    all_gather x1, waiting for transfers between devices, local(): lax.all_gather(w_in, 'fsdp', axis=0, tiled=True)  39.1 us
    all_gather x1, waiting for transfers between devices, local(): lax.all_gather(w_out, 'fsdp', axis=0, tiled=True)  25.5 us
    all_gather x1, waiting for transfers between devices, local(): lax.all_gather(part_in, 'seq', axis=0, tiled=True)  21 us
  transfers between devices with their start and end apart: 10, of which 10 were waited for; matrix products, arithmetic and copies ran while one was open for 11% of the time, Pallas kernels for 0%

profile of v1, /device:TPU:0, one launch (start us, length us, event | category | flops | bytes accessed | tf_op | source)
XLA Modules:
  0.0 581.2 jit_solution(7598705660194259229)
XLA Ops:
  8.6 39.1 %all-gather.8.cloned.1.call-done = bf16[1024,1024]{1,0:T(8,128)(2,1)} async-done(((bf16[256,1024]{1,0:T(8,128)(2,1)}), bf16[1024,1024]{1,0:T(8,128)(2,1)}) %all-gather.8.cloned.1.call-update) | async-done | bytes 2097168 | tf_op jit(solution)/shard_map/all_gather | solution.py:76
  47.8 4.6 fusion.26
  52.4 2.4 copy.26
  54.7 4.6 all-to-all-start.1
  59.3 25.5 %all-gather.6.cloned.1.call-done = bf16[1024,1024]{1,0:T(8,128)(2,1)} async-done(((bf16[256,1024]{1,0:T(8,128)(2,1)}), bf16[1024,1024]{1,0:T(8,128)(2,1)}) %all-gather.6.cloned.1.call-update) | async-done | bytes 2097168 | tf_op jit(solution)/shard_map/all_gather | solution.py:80
  84.8 5.9 %fusion.23 = bf16[1024,1024]{0,1:T(8,128)(2,1)} fusion(bf16[1024,1024]{1,0:T(8,128)(2,1)} %all-gather.6.cloned.1.call-done, bf16[1,1024,1024]{2,1,0:T(8,128)(2,1)} %param.8), kind=kOutput, calls=%fused_computation.51 | convolution fusion | flops 2148532224 | bytes 6291456 | tf_op jit(solution)/shard_map/dot_general | solution.py:78
  90.7 17.6 %all-to-all-done.1 = bf16[1024,8,128]{2,0,1:T(8,128)(2,1)S(1)} async-done(((bf16[1024,8,128]{2,0,1:T(8,128)(2,1)}), bf16[1024,8,128]{2,0,1:T(8,128)(2,1)S(1)}, u32[]{:S(2)}, u32[]{:S(2)}) %all-to-all-start.1) | async-done | bytes 2097184 | tf_op jit(solution)/shard_map/all_to_all | solution.py:85
  108.4 4.7 all-to-all-start
  117.1 2.7 fusion.52
  119.8 42.1 %all-to-all-done = bf16[1024,8,128]{0,2,1:T(8,128)(2,1)} async-done(((bf16[1024,8,128]{0,2,1:T(8,128)(2,1)}), bf16[1024,8,128]{0,2,1:T(8,128)(2,1)}, u32[]{:S(2)}, u32[]{:S(2)}) %all-to-all-start) | async-done | bytes 2097184 | tf_op jit(solution)/shard_map/all_to_all | solution.py:86
  164.8 8.6 %pad_dynamic-slice_fusion.1 = (bf16[8192,64]{1,0:T(8,128)(2,1)S(1)}, bf16[8192,64]{1,0:T(8,128)(2,1)S(1)}) fusion(s32[]{:T(128)S(6)} %select_n.14, bf16[8192,64]{1,0:T(8,128)(2,1)S(1)} %copy-done, s32[]{:T(128)S(6)} %select_n.12, bf16[8192,64]{1,0:T(8,128)(2,1)S(1)} %copy-done.1), kind=kLoop, calls=%fused_computation.14 | loop fusion | bytes 4194312 | tf_op jit(solution)/shard_map/dynamic_slice | solution.py:19
  176.9 3.7 multiply_convert_fusion.3
  182.3 4.3 all-to-all-start.3
  190.7 3.1 pad_maximum_fusion.1
  193.8 41.9 %all-to-all-done.3 = bf16[8,1024,128]{1,2,0:T(8,128)(2,1)} async-done(((bf16[8,1024,128]{1,2,0:T(8,128)(2,1)}), bf16[8,1024,128]{1,2,0:T(8,128)(2,1)}, u32[]{:S(2)}, u32[]{:S(2)}) %all-to-all-start.3) | async-done | bytes 2097184 | tf_op jit(solution)/shard_map/all_to_all | solution.py:120
  237.9 4.3 fusion.19
  242.3 2.4 pad_dynamic-slice_fusion.2
  249.7 4.4 all-to-all-start.2
  254.1 4.0 copy.28
  258.1 3.3 copy.29
  261.4 49.1 %all-to-all-done.2 = bf16[8,1024,128]{1,2,0:T(8,128)(2,1)} async-done(((bf16[8,1024,128]{1,2,0:T(8,128)(2,1)}), bf16[8,1024,128]{1,2,0:T(8,128)(2,1)}, u32[]{:S(2)}, u32[]{:S(2)}) %all-to-all-start.2) | async-done | bytes 2097184 | tf_op jit(solution)/shard_map/all_to_all | solution.py:121
  310.5 6.6 %convolution_bitcast_fusion = f32[1024,1024]{0,1:T(8,128)} fusion(bf16[1024,1024]{0,1:T(8,128)(2,1)} %bitcast.20, bf16[1024,1024]{0,1:T(8,128)(2,1)} %bitcast.93), kind=kOutput, calls=%fused_computation.17 | convolution fusion | flops 2147483648 | bytes 8388608 | tf_op jit(solution)/shard_map/dot_general | solution.py:59
  317.1 5.5 copy.36
  322.7 63.7 %reduce-scatter.9.cloned.1.call-done = f32[32,1024]{1,0:T(8,128)} async-done(((f32[1024,1024]{1,0:T(8,128)}), f32[32,1024]{1,0:T(8,128)}) %reduce-scatter.9.cloned.1.call-update) | async-done | bytes 131088 | tf_op jit(solution)/shard_map/reduce_scatter | solution.py:132
  386.8 4.5 fusion.31
  392.9 135.8 %reduce-scatter.7.cloned.1.call-done = f32[32,1024]{1,0:T(8,128)} async-done(((f32[1024,1024]{1,0:T(8,128)}), f32[32,1024]{1,0:T(8,128)}) %reduce-scatter.7.cloned.1.call-update) | async-done | bytes 131088 | tf_op jit(solution)/shard_map/reduce_scatter | solution.py:135
  528.8 8.5 %all-gather = f32[8,128,128]{2,1,0:T(8,128)S(1)} all-gather(f32[2,128,128]{2,1,0:T(8,128)S(1)} %pad_maximum_fusion.10), channel_id=2, replica_groups=mesh['seq'=8,'fsdp'=4] {'fsdp'}, dimensions={0}, use_global_device_ids=true | all-gather | bytes 655360 | tf_op jit(solution)/shard_map/all_gather | solution.py:11
  538.0 6.6 %fusion.10 = bf16[1,1024,1024]{2,1,0:T(8,128)(2,1)} fusion(bf16[1,1024,1024]{2,1,0:T(8,128)(2,1)} %param.8, bf16[1024,1024]{0,1:T(8,128)(2,1)} %bitcast.20, bf16[1024,1024]{1,0:T(8,128)(2,1)} %all-gather.8.cloned.1.call-done), kind=kOutput, calls=%fused_computation.18 | convolution fusion | flops 2150629376 | bytes 8388608 | tf_op jit(solution)/shard_map/dot_general | solution.py:123
  544.7 4.1 all-gather.12.cloned.1.call-done
  548.7 2.3 broadcast_multiply_fusion
  551.1 21.0 %all-gather.10.cloned.1.call-done = f32[256,1024]{1,0:T(8,128)} async-done(((f32[32,1024]{1,0:T(8,128)}), f32[256,1024]{1,0:T(8,128)}) %all-gather.10.cloned.1.call-update) | async-done | bytes 1048592 | tf_op jit(solution)/shard_map/all_gather | solution.py:139
  572.0 2.3 broadcast_multiply_fusion.1
  (59 shorter events, 20.2 us)
Async XLA Ops:
  7.2 40.6 %all-gather.8.cloned.1.call-start = ((), (), s32[]{:S(2)}) async-start(), calls=%async_computation.7 | async-start | bytes 2621440 | tf_op jit(solution)/shard_map/all_gather | solution.py:76
  7.9 76.9 %all-gather.6.cloned.1.call-start = ((), (), s32[]{:S(2)}) async-start(), calls=%async_computation.6 | async-start | bytes 2621440 | tf_op jit(solution)/shard_map/all_gather | solution.py:80
  54.7 53.6 %all-to-all-start.1 = ((bf16[1024,8,128]{2,0,1:T(8,128)(2,1)}), bf16[1024,8,128]{2,0,1:T(8,128)(2,1)S(1)}, u32[]{:S(2)}, u32[]{:S(2)}) async-start(bf16[1024,8,128]{2,0,1:T(8,128)(2,1)} %copy.26), calls=%async_computation.1 | async-start | bytes 4194304 | tf_op jit(solution)/shard_map/all_to_all | solution.py:85
  108.4 4.7 copy-start.10
  108.4 8.6 %copy-start.9 = (bf16[2,128,128]{2,1,0:T(8,128)(2,1)S(1)}, bf16[2,128,128]{2,1,0:T(8,128)(2,1)}, u32[]{:S(2)}) copy-start(bf16[2,128,128]{2,1,0:T(8,128)(2,1)} %param.10) | copy-start | bytes 196612
  108.4 53.5 %all-to-all-start = ((bf16[1024,8,128]{0,2,1:T(8,128)(2,1)}), bf16[1024,8,128]{0,2,1:T(8,128)(2,1)}, u32[]{:S(2)}, u32[]{:S(2)}) async-start(bf16[1024,8,128]{0,2,1:T(8,128)(2,1)} %bitcast.92), calls=%async_computation | async-start | bytes 4194304 | tf_op jit(solution)/shard_map/all_to_all | solution.py:86
  161.9 2.2 copy-start
  161.9 2.9 copy-start.1
  173.4 1.3 copy-start.4
  173.4 2.0 copy-start.2
  182.3 53.4 %all-to-all-start.3 = ((bf16[8,1024,128]{1,2,0:T(8,128)(2,1)}), bf16[8,1024,128]{1,2,0:T(8,128)(2,1)}, u32[]{:S(2)}, u32[]{:S(2)}) async-start(bf16[8,1024,128]{1,2,0:T(8,128)(2,1)} %bitcast.85), calls=%async_computation.3 | async-start | bytes 4194304 | tf_op jit(solution)/shard_map/all_to_all | solution.py:120
  186.6 199.8 %reduce-scatter.9.cloned.1.call-start = ((), (), s32[]{:S(2)}) async-start(), calls=%async_computation.11 | async-start | bytes 4325376 | tf_op jit(solution)/shard_map/reduce_scatter | solution.py:132
  235.7 2.2 copy-start.11
  242.2 2.5 copy-start.7
  242.2 2.5 copy-start.8
  244.7 1.2 copy-start.5
  249.7 60.8 %all-to-all-start.2 = ((bf16[8,1024,128]{1,2,0:T(8,128)(2,1)}), bf16[8,1024,128]{1,2,0:T(8,128)(2,1)}, u32[]{:S(2)}, u32[]{:S(2)}) async-start(bf16[8,1024,128]{1,2,0:T(8,128)(2,1)} %bitcast.86), calls=%async_computation.2 | async-start | bytes 4194304 | tf_op jit(solution)/shard_map/all_to_all | solution.py:121
  254.1 274.6 %reduce-scatter.7.cloned.1.call-start = ((), (), s32[]{:S(2)}) async-start(), calls=%async_computation.10 | async-start | bytes 4325376 | tf_op jit(solution)/shard_map/reduce_scatter | solution.py:135
  322.7 226.1 %all-gather.12.cloned.1.call-start = ((), (), s32[]{:S(2)}) async-start(), calls=%async_computation.9 | async-start | bytes 1179648 | tf_op jit(solution)/shard_map/all_gather | solution.py:140
  386.5 185.6 %all-gather.10.cloned.1.call-start = ((), (), s32[]{:S(2)}) async-start(), calls=%async_computation.8 | async-start | bytes 1179648 | tf_op jit(solution)/shard_map/all_gather | solution.py:139
  386.8 4.5 copy-start.3
  386.8 4.5 copy-start.6
Sparse Core Ops, SparseCore 0:
  9.8 37.8 all-gather.7
  49.6 35.1 all-gather.5
  242.3 144.0 reduce-scatter.8
  388.6 140.0 reduce-scatter.6
  530.2 18.5 all-gather.11
  550.2 21.8 all-gather.9
